TPU v7x, 128 devices: a whole 4x4x4 slice. The times are simulated.
128 devices in a mesh: row: 8 (over z, y_hi), col: 4 (over y_lo, core), feat: 4 (over x).
Axes of the slice: x: 4, y: 4 (y_hi: 2, y_lo: 2; y = y_hi * 2 + y_lo), z: 4, core: 2. Of those that a mesh axis runs over, the one named last changes fastest.
Arguments:
- features: bfloat16 [262144, 128], P(('row', 'col'), 'feat'), may hold values from -6 to 6
- tiles: bfloat16 [8, 4, 1536, 128, 128], P('row', 'col', 'feat'), may hold values from 0 to 0.04321289
- tile_row: int32 [8, 4, 1536], P('row', 'col', 'feat'), may hold values from 0 to 255
- tile_col: int32 [8, 4, 1536], P('row', 'col', 'feat'), may hold values from 0 to 511
- tile_count: int32 [8, 4, 4], P('row', 'col', 'feat'), may hold values from 1 to 384, as said below
- weight: bfloat16 [128, 256], replicated, may hold values from -0.5 to 0.5
- bias: float32 [256], replicated, may hold values from -3 to 3
Outputs:
- output: bfloat16 [262144, 256], P(('row', 'col', 'feat'))
Inputs may be any that keep to these rules, and one draw needn't show every extreme that they name: `tile_count`: some device has all 384 slots live.
All inputs are finite; a program needn't handle non-finite values.
Results may differ from a plain program's by a relative error of at most 0.02.
Values may be sent and summed in bfloat16 or wider, within the bound.
No kernel may reach another device: no remote copies, remote signals or barrier semaphores. Data moves between devices by JAX's collectives and lax.ppermute only.
A program may use at most 128 MiB of HBM per device.

v0:
```python
import jax
import jax.numpy as jnp
from jax import lax
from jax.sharding import PartitionSpec as P


def body(features, tiles, tile_row, tile_col, tile_count, weight, bias):
    node_rows = lax.all_to_all(features, "feat", split_axis=0, concat_axis=1, tiled=True)
    sources = lax.all_gather(node_rows, ("row", "feat"), axis=0, tiled=True)
    tile_side = tiles.shape[-1]
    width = sources.shape[1]
    node_dev = features.shape[0] // lax.axis_size("feat")
    block_rows = lax.axis_size("col") * lax.axis_size("feat") * node_dev // tile_side
    src_blocks = sources.reshape(-1, tile_side, width)
    slot_total = tiles.shape[2]
    tile_stack = tiles.reshape(slot_total, tile_side, tile_side)
    row_index = tile_row.reshape(slot_total)
    col_index = tile_col.reshape(slot_total)
    live_count = tile_count.reshape(())
    block = min(32, slot_total)
    turns = (live_count + block - 1) // block

    def one_turn(turn, partial_value):
        start = turn * block
        tile_block = lax.dynamic_slice_in_dim(tile_stack, start, block, 0)
        rows_here = lax.dynamic_slice_in_dim(row_index, start, block, 0)
        cols_here = lax.dynamic_slice_in_dim(col_index, start, block, 0)
        picked = jnp.take(src_blocks, cols_here, axis=0)
        prods = jnp.einsum("tij,tjf->tif", tile_block, picked, preferred_element_type=jnp.float32)
        live = start + jnp.arange(block, dtype=jnp.int32) < live_count
        prods = jnp.where(live[:, None, None], prods, jnp.zeros_like(prods))
        return partial_value.at[rows_here].add(prods)

    empty = jnp.zeros((block_rows, tile_side, width), jnp.float32)
    partial_value = lax.fori_loop(0, turns, one_turn, empty)
    rounded = lax.optimization_barrier(
        partial_value.reshape(block_rows * tile_side, width).astype(jnp.bfloat16)
    )
    terms = rounded.astype(jnp.float32)
    agg = lax.psum_scatter(
        terms.astype(jnp.bfloat16), ("col", "feat"), scatter_dimension=0, tiled=True
    )
    hidden = jnp.dot(agg, weight, preferred_element_type=jnp.float32) + bias
    return jax.nn.relu(hidden).astype(jnp.bfloat16)


def solution(mesh):
    placed = (
        P(("row", "col"), "feat"),
        P("row", "col", "feat", None, None),
        P("row", "col", "feat"),
        P("row", "col", "feat"),
        P("row", "col", "feat"),
        P(),
        P(),
    )
    return jax.shard_map(
        body, mesh=mesh, in_specs=placed, out_specs=P(("row", "col", "feat"), None), check_vma=False
    )
```

profile of v0, /device:TPU:1, one launch (start us, length us, event | category | flops | bytes accessed | tf_op | source)
XLA Modules:
  0.0 501.4 jit_solution(782019901176667349)
XLA Ops:
  6.5 1.1 copy.17
  7.7 13.3 %all_to_all.19 = bf16[4,2048,32]{1,2,0:T(8,128)(2,1)} all-to-all(bf16[4,2048,32]{1,2,0:T(8,128)(2,1)S(1)} %bitcast.18), channel_id=1, replica_groups=mesh['row'=8,'col'=4,'feat'=4] {'feat'}, dimensions={0} | all-to-all | bytes 1048576 | tf_op jit(solution)/shard_map/all_to_all | solution.py:8
  23.1 150.9 %all-gather.2.cloned.1.call-done = bf16[65536,128]{0,1:T(8,128)(2,1)} async-done(((bf16[2048,128]{0,1:T(8,128)(2,1)}), bf16[65536,128]{0,1:T(8,128)(2,1)}) %all-gather.2.cloned.1.call-update) | async-done | bytes 16777232 | tf_op jit(solution)/shard_map/all_gather | solution.py:9
  174.0 22.4 %copy.14 = bf16[65536,128]{1,0:T(8,128)(2,1)} copy(bf16[65536,128]{0,1:T(8,128)(2,1)} %all-gather.2.cloned.1.call-done) | data formatting | bytes 33554432 | tf_op jit(solution)/shard_map/while | solution.py:35
  196.4 7.8 %broadcast_in_dim.28 = f32[256,128,128]{2,1,0:T(8,128)} broadcast(f32[]{:T(128)} %constant.47.clone.1), dimensions={} | broadcast | bytes 16777220 | tf_op jit(solution)/shard_map/broadcast_in_dim | solution.py:34
  204.3 106.8 %while.10 = (s32[]{:T(128)}, f32[256,128,128]{2,1,0:T(8,128)}, s32[]{:T(128)}, s32[384]{0:T(512)S(1)}, s32[]{:T(128)}, /*index=5*/bf16[384,128,128]{2,1,0:T(8,12...) while((s32[]{:T(128)}, f32[256,128,128]{2,1,0:T(8,128)}, ...), condition=%wide.region_2.3_spmd, body=%wide.region_0.2_spmd.sunk | while | flops 135791968 | bytes 12588215 | solution.py:35
  205.1 6.5 %gather_fusion = bf16[32,128,128]{2,1,0:T(8,128)(2,1)S(1)} fusion(bf16[512,128,128]{2,1,0:T(8,128)(2,1)} %get-tuple-element.179, s32[1024]{0:T(1024)S(1)} %pad_clamp_fusion.2), kind=kCustom, calls=%fused_computation.clone.1 | custom fusion | bytes 2097280 | tf_op jit(solution)/shard_map/while/body/jit(_take)/gather | solution.py:28
  211.6 1.7 convolution_select_fusion.2
  213.4 6.2 %scatter_fusion = f32[256,128,128]{2,1,0:T(8,128)} fusion(f32[256,128,128]{2,1,0:T(8,128)} %get-tuple-element.161, s32[32]{0:T(128)S(1)} %compare_select_fusion.4, f32[32,128,128]{2,1,0:T(8,128)S(1)} %convolution_select_fusion.2), kind=kCustom, calls=%fused_computation.1.clone.1 | custom fusion | flops 524288 | bytes 6291584 | tf_op jit(solution)/shard_map/while/body/scatter-add | solution.py:32
  219.7 0.7 compare_and_fusion.2
  220.4 6.5 %gather_fusion = bf16[32,128,128]{2,1,0:T(8,128)(2,1)S(1)} fusion(bf16[512,128,128]{2,1,0:T(8,128)(2,1)} %get-tuple-element.179, s32[1024]{0:T(1024)S(1)} %pad_clamp_fusion.2), kind=kCustom, calls=%fused_computation.clone.1 | custom fusion | bytes 2097280 | tf_op jit(solution)/shard_map/while/body/jit(_take)/gather | solution.py:28
  226.9 1.7 convolution_select_fusion.2
  228.7 6.2 %scatter_fusion = f32[256,128,128]{2,1,0:T(8,128)} fusion(f32[256,128,128]{2,1,0:T(8,128)} %get-tuple-element.161, s32[32]{0:T(128)S(1)} %compare_select_fusion.4, f32[32,128,128]{2,1,0:T(8,128)S(1)} %convolution_select_fusion.2), kind=kCustom, calls=%fused_computation.1.clone.1 | custom fusion | flops 524288 | bytes 6291584 | tf_op jit(solution)/shard_map/while/body/scatter-add | solution.py:32
  235.7 6.5 %gather_fusion = bf16[32,128,128]{2,1,0:T(8,128)(2,1)S(1)} fusion(bf16[512,128,128]{2,1,0:T(8,128)(2,1)} %get-tuple-element.179, s32[1024]{0:T(1024)S(1)} %pad_clamp_fusion.2), kind=kCustom, calls=%fused_computation.clone.1 | custom fusion | bytes 2097280 | tf_op jit(solution)/shard_map/while/body/jit(_take)/gather | solution.py:28
  242.2 1.7 convolution_select_fusion.2
  244.0 6.1 %scatter_fusion = f32[256,128,128]{2,1,0:T(8,128)} fusion(f32[256,128,128]{2,1,0:T(8,128)} %get-tuple-element.161, s32[32]{0:T(128)S(1)} %compare_select_fusion.4, f32[32,128,128]{2,1,0:T(8,128)S(1)} %convolution_select_fusion.2), kind=kCustom, calls=%fused_computation.1.clone.1 | custom fusion | flops 524288 | bytes 6291584 | tf_op jit(solution)/shard_map/while/body/scatter-add | solution.py:32
  250.2 0.7 compare_and_fusion.2
  250.9 6.5 %gather_fusion = bf16[32,128,128]{2,1,0:T(8,128)(2,1)S(1)} fusion(bf16[512,128,128]{2,1,0:T(8,128)(2,1)} %get-tuple-element.179, s32[1024]{0:T(1024)S(1)} %pad_clamp_fusion.2), kind=kCustom, calls=%fused_computation.clone.1 | custom fusion | bytes 2097280 | tf_op jit(solution)/shard_map/while/body/jit(_take)/gather | solution.py:28
  257.4 1.7 convolution_select_fusion.2
  259.2 6.2 %scatter_fusion = f32[256,128,128]{2,1,0:T(8,128)} fusion(f32[256,128,128]{2,1,0:T(8,128)} %get-tuple-element.161, s32[32]{0:T(128)S(1)} %compare_select_fusion.4, f32[32,128,128]{2,1,0:T(8,128)S(1)} %convolution_select_fusion.2), kind=kCustom, calls=%fused_computation.1.clone.1 | custom fusion | flops 524288 | bytes 6291584 | tf_op jit(solution)/shard_map/while/body/scatter-add | solution.py:32
  266.2 6.5 %gather_fusion = bf16[32,128,128]{2,1,0:T(8,128)(2,1)S(1)} fusion(bf16[512,128,128]{2,1,0:T(8,128)(2,1)} %get-tuple-element.179, s32[1024]{0:T(1024)S(1)} %pad_clamp_fusion.2), kind=kCustom, calls=%fused_computation.clone.1 | custom fusion | bytes 2097280 | tf_op jit(solution)/shard_map/while/body/jit(_take)/gather | solution.py:28
  272.8 1.7 convolution_select_fusion.2
  274.5 6.2 %scatter_fusion = f32[256,128,128]{2,1,0:T(8,128)} fusion(f32[256,128,128]{2,1,0:T(8,128)} %get-tuple-element.161, s32[32]{0:T(128)S(1)} %compare_select_fusion.4, f32[32,128,128]{2,1,0:T(8,128)S(1)} %convolution_select_fusion.2), kind=kCustom, calls=%fused_computation.1.clone.1 | custom fusion | flops 524288 | bytes 6291584 | tf_op jit(solution)/shard_map/while/body/scatter-add | solution.py:32
  281.5 6.5 %gather_fusion = bf16[32,128,128]{2,1,0:T(8,128)(2,1)S(1)} fusion(bf16[512,128,128]{2,1,0:T(8,128)(2,1)} %get-tuple-element.179, s32[1024]{0:T(1024)S(1)} %pad_clamp_fusion.2), kind=kCustom, calls=%fused_computation.clone.1 | custom fusion | bytes 2097280 | tf_op jit(solution)/shard_map/while/body/jit(_take)/gather | solution.py:28
  288.0 1.7 convolution_select_fusion.2
  289.8 6.1 %scatter_fusion = f32[256,128,128]{2,1,0:T(8,128)} fusion(f32[256,128,128]{2,1,0:T(8,128)} %get-tuple-element.161, s32[32]{0:T(128)S(1)} %compare_select_fusion.4, f32[32,128,128]{2,1,0:T(8,128)S(1)} %convolution_select_fusion.2), kind=kCustom, calls=%fused_computation.1.clone.1 | custom fusion | flops 524288 | bytes 6291584 | tf_op jit(solution)/shard_map/while/body/scatter-add | solution.py:32
  296.7 6.5 %gather_fusion = bf16[32,128,128]{2,1,0:T(8,128)(2,1)S(1)} fusion(bf16[512,128,128]{2,1,0:T(8,128)(2,1)} %get-tuple-element.179, s32[1024]{0:T(1024)S(1)} %pad_clamp_fusion.2), kind=kCustom, calls=%fused_computation.clone.1 | custom fusion | bytes 2097280 | tf_op jit(solution)/shard_map/while/body/jit(_take)/gather | solution.py:28
  303.2 1.7 convolution_select_fusion.2
  305.0 6.1 %scatter_fusion = f32[256,128,128]{2,1,0:T(8,128)} fusion(f32[256,128,128]{2,1,0:T(8,128)} %get-tuple-element.161, s32[32]{0:T(128)S(1)} %compare_select_fusion.4, f32[32,128,128]{2,1,0:T(8,128)S(1)} %convolution_select_fusion.2), kind=kCustom, calls=%fused_computation.1.clone.1 | custom fusion | flops 524288 | bytes 6291584 | tf_op jit(solution)/shard_map/while/body/scatter-add | solution.py:32
  311.1 9.2 %convert_element_type.11 = bf16[256,128,128]{2,1,0:T(8,128)(2,1)} convert(f32[256,128,128]{2,1,0:T(8,128)} %get-tuple-element.48) | non-fusion elementwise | flops 4194304 | bytes 25165824 | tf_op jit(solution)/shard_map/convert_element_type | solution.py:37
  320.3 171.8 %reduce-scatter.2.cloned.1.call-done = bf16[2048,128]{1,0:T(8,128)(2,1)} async-done(((bf16[32768,128]{1,0:T(8,128)(2,1)}), bf16[2048,128]{1,0:T(8,128)(2,1)}) %reduce-scatter.2.cloned.1.call-update) | async-done | bytes 524304 | tf_op jit(solution)/shard_map/reduce_scatter | solution.py:40
  492.2 2.4 fusion.7
  (29 shorter events, 5.7 us)
Async XLA Ops:
  6.5 485.6 %copy-start = (bf16[128,256]{1,0:T(8,128)(2,1)S(1)}, bf16[128,256]{1,0:T(8,128)(2,1)}, u32[]{:S(2)}) copy-start(bf16[128,256]{1,0:T(8,128)(2,1)} %param.14) | copy-start | bytes 196612
  6.5 167.5 %all-gather.2.cloned.1.call-start = ((), (), s32[]{:S(2)}) async-start(), calls=%async_computation.2 | async-start | bytes 17301504 | tf_op jit(solution)/shard_map/all_gather | solution.py:9
  21.0 471.2 %reduce-scatter.2.cloned.1.call-start = ((), (), s32[]{:S(2)}) async-start(), calls=%async_computation.3 | async-start | bytes 8912896 | tf_op jit(solution)/shard_map/reduce_scatter | solution.py:40
  311.1 181.1 %copy-start.1 = (f32[256]{0:T(256)S(1)}, f32[256]{0:T(256)}, u32[]{:S(2)}) copy-start(f32[256]{0:T(256)} %param.15) | copy-start | bytes 3076
Sparse Core Ops, SparseCore 0:
  21.1 152.8 all-gather.1
  320.5 171.6 reduce-scatter.1
where the time goes:
time: 505 us; the launch traced here: 501 us
  waiting for transfers between devices  323 us (64%)
  local copies, waits for them, and re-layouts  77 us (15%)
  other arithmetic  59.5 us (12%)
  matrix products  14.6 us (3%)
  between operations  14.1 us (3%)
  blocking collectives  13.3 us (3%)
    reduce_scatter x1, waiting for transfers between devices, body(): lax.psum_scatter(terms.astype(jnp.bfloat16), ('col', 'feat'), scatter_dim...  172 us
    all_gather x1, waiting for transfers between devices, body(): sources = lax.all_gather(node_rows, ('row', 'feat'), axis=0, tiled=True)  151 us
    gather x7, local copies, waits for them, and re-layouts, one_turn(): picked = jnp.take(src_blocks, cols_here, axis=0)  45.6 us
    scatter-add x7, other arithmetic, one_turn(): return partial_value.at[rows_here].add(prods)  43.3 us
    while x1, local copies, waits for them, and re-layouts, body(): partial_value = lax.fori_loop(0, turns, one_turn, empty)  22.4 us
    all_to_all x1, blocking collectives, body(): lax.all_to_all(features, 'feat', split_axis=0, concat_axis=1, tiled=True)  13.3 us
    dot_general x7, matrix products, one_turn(): jnp.einsum('tij,tjf->tif', tile_block, picked, preferred_element_type=jnp...  12.2 us
  transfers between devices with their start and end apart: 2, of which 2 were waited for; matrix products, arithmetic and copies ran while one was open for 0% of the time, Pallas kernels for 0%

commit v1 on v0

--- a/solution.py
+++ b/solution.py
@@ -4,8 +4,15 @@
 from jax.sharding import PartitionSpec as P
 
 
+def swap_blocks(x, mesh_axis, split, join):
+    count = lax.axis_size(mesh_axis)
+    blocks = jnp.stack(jnp.split(x, count, axis=split), axis=0)
+    blocks = lax.all_to_all(blocks, mesh_axis, split_axis=0, concat_axis=0)
+    return jnp.concatenate(blocks, axis=join)
+
+
 def body(features, tiles, tile_row, tile_col, tile_count, weight, bias):
-    node_rows = lax.all_to_all(features, "feat", split_axis=0, concat_axis=1, tiled=True)
+    node_rows = swap_blocks(features, "feat", 0, 1)
     sources = lax.all_gather(node_rows, ("row", "feat"), axis=0, tiled=True)
     tile_side = tiles.shape[-1]
     width = sources.shape[1]

time: 505 us -> 486 us (0.962)
  local copies, waits for them, and re-layouts: 77 us -> 55.6 us
    while x1 -> x0, local copies, waits for them, and re-layouts: 22.4 us -> none  [body(): partial_value = lax.fori_loop(0, turns, one_turn, empty)]
where the time goes in v1:
time: 486 us; the launch traced here: 484 us
  waiting for transfers between devices  326 us (67%)
  other arithmetic  59.6 us (12%)
  local copies, waits for them, and re-layouts  55.6 us (11%)
  matrix products  14.6 us (3%)
  between operations  14.1 us (3%)
  blocking collectives  13.2 us (3%)
    reduce_scatter x1, waiting for transfers between devices, body(): lax.psum_scatter(terms.astype(jnp.bfloat16), ('col', 'feat'), scatter_dim...  172 us
    all_gather x1, waiting for transfers between devices, body(): sources = lax.all_gather(node_rows, ('row', 'feat'), axis=0, tiled=True)  154 us
    gather x7, local copies, waits for them, and re-layouts, one_turn(): picked = jnp.take(src_blocks, cols_here, axis=0)  45.6 us
    scatter-add x7, other arithmetic, one_turn(): return partial_value.at[rows_here].add(prods)  43.3 us
    all_to_all x1, blocking collectives, swap_blocks(): blocks = lax.all_to_all(blocks, mesh_axis, split_axis=0, concat_axis=0)  13.2 us
    dot_general x7, matrix products, one_turn(): jnp.einsum('tij,tjf->tif', tile_block, picked, preferred_element_type=jnp...  12.2 us
  transfers between devices with their start and end apart: 2, of which 2 were waited for; matrix products, arithmetic and copies ran while one was open for 0% of the time, Pallas kernels for 0%

profile of v1, /device:TPU:1, one launch (start us, length us, event | category | flops | bytes accessed | tf_op | source)
XLA Modules:
  0.0 483.6 jit_solution(10772969125299611784)
XLA Ops:
  6.5 1.2 slice_bitcast_fusion.3
  7.8 13.2 %all_to_all.5 = bf16[4,2048,32]{1,2,0:T(8,128)(2,1)S(1)} all-to-all(bf16[4,2048,32]{1,2,0:T(8,128)(2,1)S(1)} %pad_maximum_fusion), channel_id=1, replica_groups=mesh['row'=8,'col'=4,'feat'=4] {'feat'}, dimensions={0} | all-to-all | bytes 1048576 | tf_op jit(solution)/shard_map/all_to_all | solution.py:10
  21.0 1.0 copy.8
  24.1 154.5 %all-gather.2.cloned.1.call-done = bf16[65536,128]{1,0:T(8,128)(2,1)} async-done(((bf16[2048,128]{1,0:T(8,128)(2,1)}), bf16[65536,128]{1,0:T(8,128)(2,1)}) %all-gather.2.cloned.1.call-update) | async-done | bytes 16777232 | tf_op jit(solution)/shard_map/all_gather | solution.py:16
  178.6 7.8 %broadcast_in_dim.28 = f32[256,128,128]{2,1,0:T(8,128)} broadcast(f32[]{:T(128)} %constant.47.clone.1), dimensions={} | broadcast | bytes 16777220 | tf_op jit(solution)/shard_map/broadcast_in_dim | solution.py:41
  186.5 106.8 %while.10 = (s32[]{:T(128)}, f32[256,128,128]{2,1,0:T(8,128)}, s32[]{:T(128)}, s32[384]{0:T(512)S(1)}, s32[]{:T(128)}, /*index=5*/bf16[384,128,128]{2,1,0:T(8,12...) while((s32[]{:T(128)}, f32[256,128,128]{2,1,0:T(8,128)}, ...), condition=%wide.region_2.3_spmd, body=%wide.region_0.2_spmd.sunk | while | flops 135791968 | bytes 12588215 | solution.py:42
  186.6 0.7 compare_and_fusion.2
  187.3 6.5 %gather_fusion = bf16[32,128,128]{2,1,0:T(8,128)(2,1)S(1)} fusion(bf16[512,128,128]{2,1,0:T(8,128)(2,1)} %get-tuple-element.159, s32[1024]{0:T(1024)S(1)} %pad_clamp_fusion.2), kind=kCustom, calls=%fused_computation.clone.1 | custom fusion | bytes 2097280 | tf_op jit(solution)/shard_map/while/body/jit(_take)/gather | solution.py:35
  193.8 1.7 convolution_select_fusion.2
  195.6 6.2 %scatter_fusion = f32[256,128,128]{2,1,0:T(8,128)} fusion(f32[256,128,128]{2,1,0:T(8,128)} %get-tuple-element.141, s32[32]{0:T(128)S(1)} %compare_select_fusion.4, f32[32,128,128]{2,1,0:T(8,128)S(1)} %convolution_select_fusion.2), kind=kCustom, calls=%fused_computation.1.clone.1 | custom fusion | flops 524288 | bytes 6291584 | tf_op jit(solution)/shard_map/while/body/scatter-add | solution.py:39
  201.9 0.7 compare_and_fusion.2
  202.6 6.5 %gather_fusion = bf16[32,128,128]{2,1,0:T(8,128)(2,1)S(1)} fusion(bf16[512,128,128]{2,1,0:T(8,128)(2,1)} %get-tuple-element.159, s32[1024]{0:T(1024)S(1)} %pad_clamp_fusion.2), kind=kCustom, calls=%fused_computation.clone.1 | custom fusion | bytes 2097280 | tf_op jit(solution)/shard_map/while/body/jit(_take)/gather | solution.py:35
  209.1 1.7 convolution_select_fusion.2
  210.9 6.2 %scatter_fusion = f32[256,128,128]{2,1,0:T(8,128)} fusion(f32[256,128,128]{2,1,0:T(8,128)} %get-tuple-element.141, s32[32]{0:T(128)S(1)} %compare_select_fusion.4, f32[32,128,128]{2,1,0:T(8,128)S(1)} %convolution_select_fusion.2), kind=kCustom, calls=%fused_computation.1.clone.1 | custom fusion | flops 524288 | bytes 6291584 | tf_op jit(solution)/shard_map/while/body/scatter-add | solution.py:39
  217.9 6.5 %gather_fusion = bf16[32,128,128]{2,1,0:T(8,128)(2,1)S(1)} fusion(bf16[512,128,128]{2,1,0:T(8,128)(2,1)} %get-tuple-element.159, s32[1024]{0:T(1024)S(1)} %pad_clamp_fusion.2), kind=kCustom, calls=%fused_computation.clone.1 | custom fusion | bytes 2097280 | tf_op jit(solution)/shard_map/while/body/jit(_take)/gather | solution.py:35
  224.4 1.7 convolution_select_fusion.2
  226.2 6.1 %scatter_fusion = f32[256,128,128]{2,1,0:T(8,128)} fusion(f32[256,128,128]{2,1,0:T(8,128)} %get-tuple-element.141, s32[32]{0:T(128)S(1)} %compare_select_fusion.4, f32[32,128,128]{2,1,0:T(8,128)S(1)} %convolution_select_fusion.2), kind=kCustom, calls=%fused_computation.1.clone.1 | custom fusion | flops 524288 | bytes 6291584 | tf_op jit(solution)/shard_map/while/body/scatter-add | solution.py:39
  233.1 6.5 %gather_fusion = bf16[32,128,128]{2,1,0:T(8,128)(2,1)S(1)} fusion(bf16[512,128,128]{2,1,0:T(8,128)(2,1)} %get-tuple-element.159, s32[1024]{0:T(1024)S(1)} %pad_clamp_fusion.2), kind=kCustom, calls=%fused_computation.clone.1 | custom fusion | bytes 2097280 | tf_op jit(solution)/shard_map/while/body/jit(_take)/gather | solution.py:35
  239.6 1.7 convolution_select_fusion.2
  241.4 6.2 %scatter_fusion = f32[256,128,128]{2,1,0:T(8,128)} fusion(f32[256,128,128]{2,1,0:T(8,128)} %get-tuple-element.141, s32[32]{0:T(128)S(1)} %compare_select_fusion.4, f32[32,128,128]{2,1,0:T(8,128)S(1)} %convolution_select_fusion.2), kind=kCustom, calls=%fused_computation.1.clone.1 | custom fusion | flops 524288 | bytes 6291584 | tf_op jit(solution)/shard_map/while/body/scatter-add | solution.py:39
  248.4 6.5 %gather_fusion = bf16[32,128,128]{2,1,0:T(8,128)(2,1)S(1)} fusion(bf16[512,128,128]{2,1,0:T(8,128)(2,1)} %get-tuple-element.159, s32[1024]{0:T(1024)S(1)} %pad_clamp_fusion.2), kind=kCustom, calls=%fused_computation.clone.1 | custom fusion | bytes 2097280 | tf_op jit(solution)/shard_map/while/body/jit(_take)/gather | solution.py:35
  254.9 1.7 convolution_select_fusion.2
  256.7 6.2 %scatter_fusion = f32[256,128,128]{2,1,0:T(8,128)} fusion(f32[256,128,128]{2,1,0:T(8,128)} %get-tuple-element.141, s32[32]{0:T(128)S(1)} %compare_select_fusion.4, f32[32,128,128]{2,1,0:T(8,128)S(1)} %convolution_select_fusion.2), kind=kCustom, calls=%fused_computation.1.clone.1 | custom fusion | flops 524288 | bytes 6291584 | tf_op jit(solution)/shard_map/while/body/scatter-add | solution.py:39
  263.7 6.5 %gather_fusion = bf16[32,128,128]{2,1,0:T(8,128)(2,1)S(1)} fusion(bf16[512,128,128]{2,1,0:T(8,128)(2,1)} %get-tuple-element.159, s32[1024]{0:T(1024)S(1)} %pad_clamp_fusion.2), kind=kCustom, calls=%fused_computation.clone.1 | custom fusion | bytes 2097280 | tf_op jit(solution)/shard_map/while/body/jit(_take)/gather | solution.py:35
  270.2 1.7 convolution_select_fusion.2
  271.9 6.1 %scatter_fusion = f32[256,128,128]{2,1,0:T(8,128)} fusion(f32[256,128,128]{2,1,0:T(8,128)} %get-tuple-element.141, s32[32]{0:T(128)S(1)} %compare_select_fusion.4, f32[32,128,128]{2,1,0:T(8,128)S(1)} %convolution_select_fusion.2), kind=kCustom, calls=%fused_computation.1.clone.1 | custom fusion | flops 524288 | bytes 6291584 | tf_op jit(solution)/shard_map/while/body/scatter-add | solution.py:39
  278.9 6.5 %gather_fusion = bf16[32,128,128]{2,1,0:T(8,128)(2,1)S(1)} fusion(bf16[512,128,128]{2,1,0:T(8,128)(2,1)} %get-tuple-element.159, s32[1024]{0:T(1024)S(1)} %pad_clamp_fusion.2), kind=kCustom, calls=%fused_computation.clone.1 | custom fusion | bytes 2097280 | tf_op jit(solution)/shard_map/while/body/jit(_take)/gather | solution.py:35
  285.4 1.7 convolution_select_fusion.2
  287.2 6.1 %scatter_fusion = f32[256,128,128]{2,1,0:T(8,128)} fusion(f32[256,128,128]{2,1,0:T(8,128)} %get-tuple-element.141, s32[32]{0:T(128)S(1)} %compare_select_fusion.4, f32[32,128,128]{2,1,0:T(8,128)S(1)} %convolution_select_fusion.2), kind=kCustom, calls=%fused_computation.1.clone.1 | custom fusion | flops 524288 | bytes 6291584 | tf_op jit(solution)/shard_map/while/body/scatter-add | solution.py:39
  293.3 9.2 %convert_element_type.11 = bf16[256,128,128]{2,1,0:T(8,128)(2,1)} convert(f32[256,128,128]{2,1,0:T(8,128)} %get-tuple-element.48) | non-fusion elementwise | flops 4194304 | bytes 25165824 | tf_op jit(solution)/shard_map/convert_element_type | solution.py:44
  302.5 171.8 %reduce-scatter.2.cloned.1.call-done = bf16[2048,128]{1,0:T(8,128)(2,1)} async-done(((bf16[32768,128]{1,0:T(8,128)(2,1)}), bf16[2048,128]{1,0:T(8,128)(2,1)}) %reduce-scatter.2.cloned.1.call-update) | async-done | bytes 524304 | tf_op jit(solution)/shard_map/reduce_scatter | solution.py:47
  474.3 2.4 fusion.7
  (30 shorter events, 5.7 us)
Async XLA Ops:
  6.5 467.8 %copy-start = (bf16[128,256]{1,0:T(8,128)(2,1)S(1)}, bf16[128,256]{1,0:T(8,128)(2,1)}, u32[]{:S(2)}) copy-start(bf16[128,256]{1,0:T(8,128)(2,1)} %param.14) | copy-start | bytes 196612
  6.5 172.1 %all-gather.2.cloned.1.call-start = ((), (), s32[]{:S(2)}) async-start(), calls=%async_computation.2 | async-start | bytes 17301504 | tf_op jit(solution)/shard_map/all_gather | solution.py:16
  22.0 452.3 %reduce-scatter.2.cloned.1.call-start = ((), (), s32[]{:S(2)}) async-start(), calls=%async_computation.3 | async-start | bytes 8912896 | tf_op jit(solution)/shard_map/reduce_scatter | solution.py:47
  302.5 171.9 %copy-start.1 = (f32[256]{0:T(256)S(1)}, f32[256]{0:T(256)}, u32[]{:S(2)}) copy-start(f32[256]{0:T(256)} %param.15) | copy-start | bytes 3076
Sparse Core Ops, SparseCore 0:
  22.1 156.4 all-gather.1
  302.6 171.6 reduce-scatter.1
